TPU v7x, 32 devices: a whole 2x2x4 slice. The times are simulated.
32 devices in a mesh: parts: 2 (over y), row: 4 (over z), frame: 4 (over x, core).
Axes of the slice: x: 2, y: 2, z: 4, core: 2. Of those that a mesh axis runs over, the one named last changes fastest.
Arguments:
- latent: bfloat16 [8, 8, 16, 512], P(('parts', 'frame'), 'row'), parts along dimension 0, may hold values from -15 to 15
- qkv_weight: bfloat16 [3, 512, 512], P(None, 'frame'), may hold values from -0.125 to 0.125
- out_weight: bfloat16 [512, 512], P('frame'), may hold values from -0.25 to 0.25
- attn_gain: float32 [512], replicated, may hold values from 0.1 to 1.9
- in_weight: bfloat16 [512, 2, 2048], P(None, None, 'frame'), may hold values from -0.25 to 0.25
- depth_weight: float32 [3, 3, 2, 2048], replicated, may hold values from -2 to 2
- down_weight: bfloat16 [2048, 512], P('frame'), may hold values from -0.125 to 0.125
- mlp_gain: float32 [512], replicated, may hold values from 0.1 to 1.9
- conv_first: bfloat16 [3, 3, 3, 512, 512], P(None, None, None, 'frame'), may hold values from -0.0546875 to 0.0546875
- conv_second: bfloat16 [3, 3, 3, 512, 512], P(None, None, None, 'frame'), may hold values from -0.0546875 to 0.0546875
Outputs:
- decoded: bfloat16 [8, 8, 16, 512], P('parts', 'row', 'frame'), parts along dimension 0
There are 2 independent parts, one for each index of `parts`. A program takes and returns all parts, laid end to end along the dimension named above; an argument that names none is the same for every part. Nothing has to cross between parts.
All inputs are finite; a program needn't handle non-finite values.
Results may differ from a plain program's by a relative error of at most 0.015.
Values may be sent and summed in bfloat16 or wider, within the bound.
A program may use at most 128 MiB of HBM per device.

v0:
```python
import jax
import jax.numpy as jnp
from jax import lax
from jax.sharding import PartitionSpec as P

HEAD = 32


def padded_2(cells, sides, width):
    for axis, dim in sides:
        count = lax.axis_size(axis)
        ends = count - 1
        head = lax.slice_in_dim(cells, 0, width, axis=dim)
        tail = lax.slice_in_dim(cells, cells.shape[dim] - width, cells.shape[dim], axis=dim)
        cells = jnp.concatenate(
            [
                lax.ppermute(tail, axis, [(i, (i + 1) % count) for i in range(ends)]),
                cells,
                lax.ppermute(head, axis, [((i + 1) % count, i) for i in range(ends)]),
            ],
            axis=dim,
        )
    return cells


def norm_rows(values, gain):
    return values * lax.rsqrt(jnp.mean(values * values, axis=-1, keepdims=True) + 1e-05) * gain


def attend(packed):
    frames, height, columns = (packed.shape[0], packed.shape[1], packed.shape[2])
    width = packed.shape[4]
    heads = width // HEAD
    flat = packed.reshape(frames, height * columns, 3, heads, HEAD)
    query = jnp.maximum(flat[:, :, 0], 0)
    keys = jnp.maximum(flat[:, :, 1], 0)
    values = flat[:, :, 2]
    state = jnp.einsum("fnhd,fnhe->fhde", keys, values, preferred_element_type=jnp.float32)
    key_total = jnp.sum(keys.astype(jnp.float32), axis=1)
    state, key_total = (
        lax.psum(state.astype(jnp.bfloat16), "row").astype(jnp.float32),
        lax.psum(key_total.astype(jnp.bfloat16), "row").astype(jnp.float32),
    )
    count = height * lax.axis_size("row") * columns
    state = state / count
    key_mean = key_total / count
    query_wide = query.astype(jnp.float32)
    numer = jnp.einsum("fnhd,fhde->fnhe", query_wide, state, precision=lax.Precision.HIGHEST)
    denom = jnp.maximum(
        jnp.einsum("fnhd,fhd->fnh", query_wide, key_mean, precision=lax.Precision.HIGHEST), 1.0
    )
    return (numer / denom[..., None]).astype(jnp.bfloat16).reshape(frames, height, columns, width)


def depth_mix(inner, depth_local):
    height, columns = (inner.shape[1], inner.shape[2])
    extended = padded_2(inner, (("row", 1),), 1)
    padded = jnp.pad(extended, ((0, 0), (0, 0), (1, 1), (0, 0), (0, 0)))
    spread = jnp.zeros(inner.shape, jnp.float32)
    for shift_row in range(3):
        for shift_col in range(3):
            spread = (
                spread
                + padded[:, shift_row : shift_row + height, shift_col : shift_col + columns].astype(
                    jnp.float32
                )
                * depth_local[shift_row, shift_col]
            )
    return (spread[..., 0, :] * jax.nn.silu(spread[..., 1, :])).astype(jnp.bfloat16)


def conv_tile(extended, kernel):
    frames, padded_rows, columns, width = extended.shape
    height = padded_rows - 2
    out_width = kernel.shape[3]
    padded = jnp.pad(extended, ((1, 1), (0, 0), (1, 1), (0, 0)))
    result = jnp.zeros((frames * height * columns, out_width), jnp.float32)
    for shift_time in range(3):
        for shift_row in range(3):
            slab = padded[shift_time : shift_time + frames, shift_row : shift_row + height]
            stacked = jnp.stack(
                [slab[:, :, shift_col : shift_col + columns] for shift_col in range(3)], axis=3
            )
            result = result + jnp.einsum(
                "nci,coi->no",
                stacked.reshape(-1, 3, width),
                kernel[shift_time, shift_row],
                preferred_element_type=jnp.float32,
            )
    return result.reshape(frames, height, columns, out_width)


def local(
    latent,
    qkv_weight,
    out_weight,
    attn_gain,
    in_weight,
    depth_weight,
    down_weight,
    mlp_gain,
    conv_first,
    conv_second,
):
    frames, height, columns, width = latent.shape
    place = lax.axis_index("frame")
    packed = jnp.einsum(
        "frwc,kjc->frwkj",
        latent,
        lax.all_gather(qkv_weight, "frame", axis=1, tiled=True),
        preferred_element_type=jnp.float32,
    ).astype(jnp.bfloat16)
    mixed = attend(packed)
    section = mixed
    attn_out = jnp.einsum(
        "frwj,jc->frwc",
        section,
        lax.all_gather(out_weight, "frame", axis=0, tiled=True),
        preferred_element_type=jnp.float32,
    )
    first = (latent.astype(jnp.float32) + norm_rows(attn_out, attn_gain)).astype(jnp.bfloat16)
    inner = jax.nn.silu(
        jnp.einsum(
            "frwc,ckj->frwkj",
            first,
            lax.all_gather(in_weight, "frame", axis=2, tiled=True),
            preferred_element_type=jnp.float32,
        )
    ).astype(jnp.bfloat16)
    gated = depth_mix(inner, depth_weight)
    section = gated
    mlp_out = jnp.einsum(
        "frwj,jc->frwc",
        section,
        lax.all_gather(down_weight, "frame", axis=0, tiled=True),
        preferred_element_type=jnp.float32,
    )
    second = (first.astype(jnp.float32) + norm_rows(mlp_out, mlp_gain)).astype(jnp.bfloat16)
    gathered = lax.all_gather(second, "frame", axis=0, tiled=True)
    out_share = conv_first.shape[3]
    extended = padded_2(gathered, (("row", 1),), 2)
    activated = jax.nn.silu(conv_tile(extended, conv_first))
    global_row = lax.axis_index("row") * height - 1 + lax.iota(jnp.int32, height + 2)
    inside = ((global_row >= 0) & (global_row < height * lax.axis_size("row"))).astype(jnp.float32)
    hidden_conv = (activated * inside[None, :, None, None]).astype(jnp.bfloat16)
    joined = lax.all_gather(hidden_conv, "frame", axis=3, tiled=True)
    result = conv_tile(joined, conv_second)
    own_part = lax.dynamic_slice_in_dim(gathered, place * out_share, out_share, 3)
    final = (own_part.astype(jnp.float32) + result).astype(jnp.bfloat16)
    return lax.all_to_all(final, "frame", split_axis=2, concat_axis=3, tiled=True)


def solution(mesh):
    in_specs = (
        P(("parts", "frame"), "row", None, None),
        P(None, "frame", None),
        P("frame", None),
        P(),
        P(None, None, "frame"),
        P(),
        P("frame", None),
        P(),
        P(None, None, None, "frame", None),
        P(None, None, None, "frame", None),
    )
    out_specs = P("parts", "row", "frame", None)
    return jax.shard_map(local, mesh=mesh, in_specs=in_specs, out_specs=out_specs, check_vma=False)
```

profile of v0, /device:TPU:0, one launch (start us, length us, event | category | flops | bytes accessed | tf_op | source)
XLA Modules:
  0.0 137.9 jit_solution(649510478248561732)
XLA Ops:
  6.5 0.7 all-gather.4.cloned.1.call-update
  7.3 0.0 all-gather.6.cloned.1.call-start
  7.3 2.4 %copy.34 = bf16[512,2,512]{2,0,1:T(8,128)(2,1)} copy(bf16[512,2,512]{2,1,0:T(2,128)(2,1)} %param.14) | data formatting | bytes 2097152 | tf_op args[4]
  9.7 0.0 all-gather.6.cloned.1.call-update
  9.7 0.0 all-gather.8.cloned.1.call-start
  9.8 0.7 all-gather.8.cloned.1.call-update
  10.5 8.6 %all_gather.19 = bf16[512,512]{1,0:T(8,128)(2,1)S(1)} all-gather(bf16[128,512]{1,0:T(8,128)(2,1)S(1)} %copy-done.1), channel_id=1, replica_groups=mesh['parts'=2,'row'=4,'frame'=4] {'frame'}, dimensions={0}, use_global_device_ids=true | all-gather | bytes 655360 | tf_op jit(solution)/shard_map/all_gather | solution.py:118
  19.1 12.1 %all-gather.4.cloned.1.call-done = bf16[3,512,512]{2,1,0:T(8,128)(2,1)} async-done(((bf16[3,128,512]{2,1,0:T(8,128)(2,1)}), bf16[3,512,512]{2,1,0:T(8,128)(2,1)}) %all-gather.4.cloned.1.call-update) | async-done | bytes 1572880 | tf_op jit(solution)/shard_map/all_gather | solution.py:110
  31.3 2.0 %fusion.7 = bf16[2,16,3,512]{3,1,2,0:T(8,128)(2,1)S(1)} fusion(bf16[3,512,512]{2,1,0:T(8,128)(2,1)} %all-gather.4.cloned.1.call-done, bf16[1,2,16,512]{3,2,1,0:T(8,128)(2,1)S(1)} %copy-done.2), kind=kOutput, calls=%fused_computation.59 | convolution fusion | flops 50380800 | bytes 1703936 | tf_op jit(solution)/shard_map/frwc,kjc->frwkj/dot_general | solution.py:107
  33.3 0.2 reshape.298
  33.5 0.2 copy.44
  33.7 0.1 maximum_reduce_fusion
  33.8 0.2 fusion.10
  34.0 21.4 %all-reduce.3 = (bf16[1,16,32,32]{3,2,1,0:T(8,128)(2,1)S(1)}, bf16[1,16,32]{2,1,0:T(8,128)(2,1)S(1)}) all-reduce(bf16[1,16,32,32]{3,2,1,0:T(8,128)(2,1)S(1)} %fusion.10, bf16[1,16,32]{2,1,0:T(8,128)(2,1)S(1)} %bitcast.373), channel_id=1, replica_groups=mesh['parts'=2,'row'=4,'frame'=4] {'row'}, use_global_device_ids=true, to_apply=%region_0.0 | all-reduce | flops 16896 | bytes 67584 | tf_op jit(solution)/shard_map/psum | solution.py:41
  55.4 0.2 copy.46
  55.6 0.2 fusion.174
  55.8 0.4 fusion.28
  56.2 0.2 copy.33
  56.4 0.2 reshape.302
  56.6 0.3 multiply_reduce_fusion.1
  56.9 0.1 fusion.184
  57.0 10.4 %all-gather.6.cloned.1.call-done = bf16[512,2,2048]{2,0,1:T(8,128)(2,1)} async-done(((bf16[512,2,512]{2,0,1:T(8,128)(2,1)}), bf16[512,2,2048]{2,0,1:T(8,128)(2,1)}) %all-gather.6.cloned.1.call-update) | async-done | bytes 4194320 | tf_op jit(solution)/shard_map/all_gather | solution.py:126
  67.3 3.0 %multiply_convert_fusion = bf16[2,16,2,2048]{3,1,2,0:T(8,128)(2,1)S(1)} fusion(bf16[512,2,2048]{2,0,1:T(8,128)(2,1)} %all-gather.6.cloned.1.call-done, bf16[1,2,16,512]{3,2,1,0:T(8,128)(2,1)S(1)} %fusion.184), kind=kOutput, calls=%fused_computation.154 | convolution fusion | flops 134873088 | bytes 4489216 | tf_op jit(solution)/shard_map/frwc,ckj->frwkj/dot_general | solution.py:123
  70.4 3.4 %collective-permute-start = (bf16[1,1,16,2,2048]{4,2,3,1,0:T(8,128)(2,1)S(1)}, bf16[1,1,16,2,2048]{4,2,3,1,0:T(8,128)(2,1)S(1)}, u32[]{:S(2)}, u32[]{:S(2)}) collective-permute-start(bf16[1,1,16,2,2048]{4,2,3,1,0:T(8,128)(2,1)S(1)} %get-tuple-element.62), channel_id=1, source_target_pairs={{0,4},{4,8},{8,12},{1,5},{5,9},{9,13},{2,6},{6,10},{10,14},{3,7},{... | collective-permute-start | bytes 393224 | tf_op jit(solution)/shard_map/ppermute | solution.py:17
  73.8 1.3 collective-permute-start.1
  75.1 1.8 %collective-permute-done = bf16[1,1,16,2,2048]{4,2,3,1,0:T(8,128)(2,1)S(1)} collective-permute-done((bf16[1,1,16,2,2048]{4,2,3,1,0:T(8,128)(2,1)S(1)}, bf16[1,1,16,2,2048]{4,2,3,1,0:T(8,128)(2,1)S(1)}, u32[]{:S(2)}, u32[]{:S(2)}) %collective-permute-start) | collective-permute-done | bytes 131104 | tf_op jit(solution)/shard_map/ppermute | solution.py:17
  76.9 4.1 %collective-permute-done.1 = bf16[1,1,16,2,2048]{4,2,3,1,0:T(8,128)(2,1)S(1)} collective-permute-done((bf16[1,1,16,2,2048]{4,2,3,1,0:T(8,128)(2,1)S(1)}, bf16[1,1,16,2,2048]{4,2,3,1,0:T(8,128)(2,1)S(1)}, u32[]{:S(2)}, u32[]{:S(2)}) %collective-permute-start.1) | collective-permute-done | bytes 131104 | tf_op jit(solution)/shard_map/ppermute | solution.py:19
  81.1 0.3 fusion.33
  81.3 0.5 fusion.82
  81.8 9.7 %all-gather.8.cloned.1.call-done = bf16[2048,512]{1,0:T(8,128)(2,1)} async-done(((bf16[512,512]{1,0:T(8,128)(2,1)}), bf16[2048,512]{1,0:T(8,128)(2,1)}) %all-gather.8.cloned.1.call-update) | async-done | bytes 2097168 | tf_op jit(solution)/shard_map/all_gather | solution.py:135
  91.5 2.1 %multiply_reduce_fusion = (f32[2,16]{1,0:T(2,128)S(1)}, f32[2,16,512]{2,1,0:T(8,128)S(1)}) fusion(bf16[2048,512]{1,0:T(8,128)(2,1)} %all-gather.8.cloned.1.call-done, f32[1,2,16,2,2048]{4,2,3,1,0:T(8,128)S(1)} %fusion.82), kind=kOutput, calls=%fused_computation.264 | convolution fusion | flops 67534816 | bytes 2687104 | tf_op jit(solution)/shard_map/frwj,jc->frwc/dot_general | solution.py:132
  93.6 0.1 fusion.183
  93.7 5.4 %all_gather.22 = bf16[4,2,16,512]{3,2,1,0:T(8,128)(2,1)S(1)} all-gather(bf16[1,2,16,512]{3,2,1,0:T(8,128)(2,1)S(1)} %fusion.183), channel_id=1, replica_groups=mesh['parts'=2,'row'=4,'frame'=4] {'frame'}, dimensions={0}, use_global_device_ids=true | all-gather | bytes 163840 | tf_op jit(solution)/shard_map/all_gather | solution.py:139
  99.1 3.4 %collective-permute-start.2 = (bf16[4,2,16,512]{3,2,1,0:T(8,128)(2,1)S(1)}, bf16[4,2,16,512]{3,2,1,0:T(8,128)(2,1)S(1)}, u32[]{:S(2)}, u32[]{:S(2)}) collective-permute-start(bf16[4,2,16,512]{3,2,1,0:T(8,128)(2,1)S(1)} %all_gather.22), channel_id=1, source_target_pairs={{0,4},{4,8},{8,12},{1,5},{5,9},{9,13},{2,6},{6,10},{10,14},{3,7},{... | collective-permute-start | bytes 393224 | tf_op jit(solution)/shard_map/ppermute | solution.py:17
  102.5 1.3 collective-permute-start.3
  103.8 1.9 %collective-permute-done.2 = bf16[4,2,16,512]{3,2,1,0:T(8,128)(2,1)S(1)} collective-permute-done((bf16[4,2,16,512]{3,2,1,0:T(8,128)(2,1)S(1)}, bf16[4,2,16,512]{3,2,1,0:T(8,128)(2,1)S(1)}, u32[]{:S(2)}, u32[]{:S(2)}) %collective-permute-start.2) | collective-permute-done | bytes 131104 | tf_op jit(solution)/shard_map/ppermute | solution.py:17
  105.8 4.1 %collective-permute-done.3 = bf16[4,2,16,512]{3,2,1,0:T(8,128)(2,1)S(1)} collective-permute-done((bf16[4,2,16,512]{3,2,1,0:T(8,128)(2,1)S(1)}, bf16[4,2,16,512]{3,2,1,0:T(8,128)(2,1)S(1)}, u32[]{:S(2)}, u32[]{:S(2)}) %collective-permute-start.3) | collective-permute-done | bytes 131104 | tf_op jit(solution)/shard_map/ppermute | solution.py:19
  109.9 0.8 pad_slice_fusion.23
  110.7 0.2 fusion.213
  110.9 1.0 copy-done.5
  111.9 0.4 convolution_bitcast_fusion.8
  112.3 0.4 convolution_bitcast_fusion.7
  112.7 0.4 convolution_bitcast_fusion.6
  113.1 0.4 convolution_bitcast_fusion.5
  113.4 0.4 convolution_bitcast_fusion.4
  113.8 0.4 convolution_bitcast_fusion.3
  114.2 0.4 convolution_bitcast_fusion.2
  114.5 0.4 convolution_bitcast_fusion.1
  114.9 0.4 fusion.18
  115.3 0.1 multiply_convert_fusion.1
  115.4 5.9 %all_gather.23 = bf16[4,4,16,512]{3,2,1,0:T(8,128)(2,1)S(1)} all-gather(bf16[4,4,16,128]{3,2,1,0:T(8,128)(2,1)S(1)} %multiply_convert_fusion.1), channel_id=1, replica_groups=mesh['parts'=2,'row'=4,'frame'=4] {'frame'}, dimensions={3}, use_global_device_ids=true | all-gather | bytes 327680 | tf_op jit(solution)/shard_map/all_gather | solution.py:146
  121.3 0.3 pad_slice_fusion.47
  121.7 0.1 fusion.215
  121.8 0.3 convolution_bitcast_fusion.17
  122.1 0.3 convolution_bitcast_fusion.16
  122.4 0.3 convolution_bitcast_fusion.15
  122.6 0.3 convolution_bitcast_fusion.14
  122.9 0.3 convolution_bitcast_fusion.13
  123.2 0.3 convolution_bitcast_fusion.12
  123.5 0.3 convolution_bitcast_fusion.11
  123.7 0.3 convolution_bitcast_fusion.10
  124.0 0.3 fusion.26
  124.4 6.3 %all_to_all.18 = bf16[4,2,16,128]{3,1,0,2:T(2,128)(2,1)S(1)} all-to-all(bf16[4,2,16,128]{3,1,0,2:T(2,128)(2,1)S(1)} %copy.36), channel_id=1, replica_groups=mesh['parts'=2,'row'=4,'frame'=4] {'frame'}, dimensions={2} | all-to-all | bytes 65536 | tf_op jit(solution)/shard_map/all_to_all | solution.py:150
  130.7 0.6 all_to_all.16
  (30 shorter events, 0.3 us)
Async XLA Ops:
  6.5 4.0 %copy-start.1 = (bf16[128,512]{1,0:T(8,128)(2,1)S(1)}, bf16[128,512]{1,0:T(8,128)(2,1)}, u32[]{:S(2)}) copy-start(bf16[128,512]{1,0:T(8,128)(2,1)} %param.12) | copy-start | bytes 393220
  6.5 24.7 %copy-start.2 = (bf16[1,2,16,512]{3,2,1,0:T(8,128)(2,1)S(1)}, bf16[1,2,16,512]{3,2,1,0:T(8,128)(2,1)}, u32[]{:S(2)}) copy-start(bf16[1,2,16,512]{3,2,1,0:T(8,128)(2,1)} %param.10) | copy-start | bytes 98308
  6.5 24.7 %all-gather.4.cloned.1.call-start = ((), (), s32[]{:S(2)}) async-start(), calls=%async_computation.1 | async-start | bytes 1966080 | tf_op jit(solution)/shard_map/all_gather | solution.py:110
  7.3 60.1 %all-gather.6.cloned.1.call-start = ((), (), s32[]{:S(2)}) async-start(), calls=%async_computation.2 | async-start | bytes 5242880 | tf_op jit(solution)/shard_map/all_gather | solution.py:126
  9.7 81.7 %all-gather.8.cloned.1.call-start = ((), (), s32[]{:S(2)}) async-start(), calls=%async_computation.3 | async-start | bytes 2621440 | tf_op jit(solution)/shard_map/all_gather | solution.py:135
  19.1 37.7 %copy-start.3 = (f32[512]{0:T(512)S(1)}, f32[512]{0:T(512)}, u32[]{:S(2)}) copy-start(f32[512]{0:T(512)} %param.13) | copy-start | bytes 6148
  56.9 18.2 %copy-start = (f32[3,3,2,2048]{3,2,1,0:T(2,128)S(1)}, f32[3,3,2,2048]{3,2,1,0:T(2,128)}, u32[]{:S(2)}) copy-start(f32[3,3,2,2048]{3,2,1,0:T(2,128)} %param.15) | copy-start | bytes 442372
  70.4 6.5 %collective-permute-start = (bf16[1,1,16,2,2048]{4,2,3,1,0:T(8,128)(2,1)S(1)}, bf16[1,1,16,2,2048]{4,2,3,1,0:T(8,128)(2,1)S(1)}, u32[]{:S(2)}, u32[]{:S(2)}) collective-permute-start(bf16[1,1,16,2,2048]{4,2,3,1,0:T(8,128)(2,1)S(1)} %get-tuple-element.62), channel_id=1, source_target_pairs={{0,4},{4,8},{8,12},{1,5},{5,9},{9,13},{2,6},{6,10},{10,14},{3,7},{... | collective-permute-start | bytes 393224 | tf_op jit(solution)/shard_map/ppermute | solution.py:17
  73.8 7.3 %collective-permute-start.1 = (bf16[1,1,16,2,2048]{4,2,3,1,0:T(8,128)(2,1)S(1)}, bf16[1,1,16,2,2048]{4,2,3,1,0:T(8,128)(2,1)S(1)}, u32[]{:S(2)}, u32[]{:S(2)}) collective-permute-start(bf16[1,1,16,2,2048]{4,2,3,1,0:T(8,128)(2,1)S(1)} %get-tuple-element.63), channel_id=1, source_target_pairs={{4,0},{8,4},{12,8},{5,1},{9,5},{13,9},{6,2},{10,6},{14,10},{7,3},{... | collective-permute-start | bytes 393224 | tf_op jit(solution)/shard_map/ppermute | solution.py:19
  75.1 18.4 %copy-start.4 = (f32[512]{0:T(512)S(1)}, f32[512]{0:T(512)}, u32[]{:S(2)}) copy-start(f32[512]{0:T(512)} %param.17) | copy-start | bytes 6148
  99.1 6.6 %collective-permute-start.2 = (bf16[4,2,16,512]{3,2,1,0:T(8,128)(2,1)S(1)}, bf16[4,2,16,512]{3,2,1,0:T(8,128)(2,1)S(1)}, u32[]{:S(2)}, u32[]{:S(2)}) collective-permute-start(bf16[4,2,16,512]{3,2,1,0:T(8,128)(2,1)S(1)} %all_gather.22), channel_id=1, source_target_pairs={{0,4},{4,8},{8,12},{1,5},{5,9},{9,13},{2,6},{6,10},{10,14},{3,7},{... | collective-permute-start | bytes 393224 | tf_op jit(solution)/shard_map/ppermute | solution.py:17
  102.5 7.4 %collective-permute-start.3 = (bf16[4,2,16,512]{3,2,1,0:T(8,128)(2,1)S(1)}, bf16[4,2,16,512]{3,2,1,0:T(8,128)(2,1)S(1)}, u32[]{:S(2)}, u32[]{:S(2)}) collective-permute-start(bf16[4,2,16,512]{3,2,1,0:T(8,128)(2,1)S(1)} %all_gather.22), channel_id=1, source_target_pairs={{4,0},{8,4},{12,8},{5,1},{9,5},{13,9},{6,2},{10,6},{14,10},{7,3},{... | collective-permute-start | bytes 393224 | tf_op jit(solution)/shard_map/ppermute | solution.py:19
  109.9 2.0 %copy-start.5 = (bf16[3,3,3,128,512]{4,3,2,1,0:T(8,128)(2,1)S(1)}, bf16[3,3,3,128,512]{4,3,2,1,0:T(8,128)(2,1)}, u32[]{:S(2)}) copy-start(bf16[3,3,3,128,512]{4,3,2,1,0:T(8,128)(2,1)} %param.18) | copy-start | bytes 10616836
  114.9 6.9 %copy-start.6 = (bf16[3,3,3,128,512]{4,3,2,1,0:T(8,128)(2,1)S(1)}, bf16[3,3,3,128,512]{4,3,2,1,0:T(8,128)(2,1)}, u32[]{:S(2)}) copy-start(bf16[3,3,3,128,512]{4,3,2,1,0:T(8,128)(2,1)} %param.19) | copy-start | bytes 10616836
Sparse Core Ops, SparseCore 0:
  8.9 22.3 all-gather.3
  32.8 34.4 all-gather.5
  68.9 22.5 all-gather.7
where the time goes:
time: 138 us
  blocking collectives  47.7 us (35%)
  waiting for transfers between devices  45.5 us (33%)
  matrix products  13.8 us (10%)
  between operations  13.6 us (10%)
  starting transfers between devices  9.45 us (7%)
  local copies, waits for them, and re-layouts  6.56 us (5%)
    psum x1, blocking collectives, attend(): lax.psum(state.astype(jnp.bfloat16), 'row').astype(jnp.float32)  21.4 us
    all_gather x1, waiting for transfers between devices, local(): lax.all_gather(qkv_weight, 'frame', axis=1, tiled=True)  12.1 us
    all_gather x1, waiting for transfers between devices, local(): lax.all_gather(in_weight, 'frame', axis=2, tiled=True)  10.4 us
    all_gather x1, waiting for transfers between devices, local(): lax.all_gather(down_weight, 'frame', axis=0, tiled=True)  9.69 us
    all_gather x1, blocking collectives, local(): lax.all_gather(out_weight, 'frame', axis=0, tiled=True)  8.65 us
    ppermute x2, waiting for transfers between devices, padded_2(): lax.ppermute(head, axis, [((i + 1) % count, i) for i in range(ends)])  8.23 us
    ppermute x2, starting transfers between devices, padded_2(): lax.ppermute(tail, axis, [(i, (i + 1) % count) for i in range(ends)])  6.78 us
    all_to_all x1, blocking collectives, local(): lax.all_to_all(final, 'frame', split_axis=2, concat_axis=3, tiled=True)  6.3 us
  transfers between devices with their start and end apart: 7, of which 7 were waited for; matrix products, arithmetic and copies ran while one was open for 8% of the time, Pallas kernels for 0%

commit v1 on v0

--- a/solution.py
+++ b/solution.py
@@ -4,6 +4,30 @@
 from jax.sharding import PartitionSpec as P
 
 HEAD = 32
+
+
+def ring_apply(x, axis, dim, work, out_dim):
+    size, index, width = (lax.axis_size(axis), lax.axis_index(axis), x.shape[dim])
+    right = [(i, (i + 1) % size) for i in range(size)]
+    behind = [(b, a) for a, b in right]
+    lower, upper = (lax.ppermute(x, axis, right), lax.ppermute(x, axis, behind))
+    made = work(x, index * width)
+    length = made.shape[out_dim]
+    out = jnp.zeros((*made.shape[:out_dim], size * length, *made.shape[out_dim + 1 :]), made.dtype)
+
+    def put(out, made, source):
+        return lax.dynamic_update_slice_in_dim(out, made, source * length, axis=out_dim)
+
+    out = put(out, made, index)
+    for step in range(1, size // 2 + 1):
+        below, above = ((index - step) % size, (index + step) % size)
+        carried = (lower, upper)
+        if step < size // 2:
+            lower, upper = (lax.ppermute(lower, axis, right), lax.ppermute(upper, axis, behind))
+        out = put(out, work(carried[0], below * width), below)
+        if 2 * step < size:
+            out = put(out, work(carried[1], above * width), above)
+    return out
 
 
 def padded_2(cells, sides, width):
@@ -104,11 +128,14 @@
 ):
     frames, height, columns, width = latent.shape
     place = lax.axis_index("frame")
-    packed = jnp.einsum(
-        "frwc,kjc->frwkj",
-        latent,
-        lax.all_gather(qkv_weight, "frame", axis=1, tiled=True),
-        preferred_element_type=jnp.float32,
+    packed = ring_apply(
+        qkv_weight,
+        "frame",
+        1,
+        lambda own_block, offset: jnp.einsum(
+            "frwc,kjc->frwkj", latent, own_block, preferred_element_type=jnp.float32
+        ),
+        4,
     ).astype(jnp.bfloat16)
     mixed = attend(packed)
     section = mixed

time: 138 us -> 130 us (0.942)
  waiting for transfers between devices: 45.5 us -> 27.2 us
  blocking collectives: 47.7 us -> 57.3 us
    ppermute x0 -> x3, waiting for transfers between devices: none -> 15.6 us  [the longest x1 15.5 us: ring_apply(): lax.ppermute(lower, axis, right)]
    all_gather x1 -> x0, waiting for transfers between devices: 12.1 us -> none  [local(): lax.all_gather(qkv_weight, 'frame', axis=1, tiled=True)]
    all_gather x1, waiting for transfers between devices: 10.4 us -> 0.02 us  [local(): lax.all_gather(in_weight, 'frame', axis=2, tiled=True)]
    all_gather x1, waiting for transfers between devices: 9.69 us -> 0.02 us  [local(): lax.all_gather(down_weight, 'frame', axis=0, tiled=True)]
    all_gather x1, blocking collectives: 8.65 us -> 16.9 us  [local(): lax.all_gather(out_weight, 'frame', axis=0, tiled=True)]
    ppermute x0 -> x3, starting transfers between devices: none -> 2.87 us  [the longest x2 2.52 us: ring_apply(): lower, upper = (lax.ppermute(x, axis, right), lax.ppermute(x, axis, behind))]
    ppermute x2, starting transfers between devices: 6.78 us -> 5.09 us  [padded_2(): lax.ppermute(tail, axis, [(i, (i + 1) % count) for i in range(ends)])]
    unnamed x19 -> x21, local copies, waits for them, and re-layouts: 3.87 us -> 3.89 us
  transfers between devices with their start and end apart: 7 -> 9, of which waited for: 7 -> 5; matrix products, arithmetic and copies ran while one was open for 8% -> 6% of each run, Pallas kernels for 0% -> 0%
where the time goes in v1:
time: 130 us
  blocking collectives  57.3 us (44%)
  waiting for transfers between devices  27.2 us (21%)
  between operations  13.9 us (11%)
  matrix products  12.9 us (10%)
  starting transfers between devices  10.6 us (8%)
  local copies, waits for them, and re-layouts  6.74 us (5%)
    psum x1, blocking collectives, attend(): lax.psum(state.astype(jnp.bfloat16), 'row').astype(jnp.float32)  22.4 us
    all_gather x1, blocking collectives, local(): lax.all_gather(out_weight, 'frame', axis=0, tiled=True)  16.9 us
    ppermute x1, waiting for transfers between devices, ring_apply(): lax.ppermute(lower, axis, right)  15.5 us
    ppermute x2, waiting for transfers between devices, padded_2(): lax.ppermute(head, axis, [((i + 1) % count, i) for i in range(ends)])  8.47 us
    all_to_all x1, blocking collectives, local(): lax.all_to_all(final, 'frame', split_axis=2, concat_axis=3, tiled=True)  6.52 us
    all_gather x1, blocking collectives, local(): joined = lax.all_gather(hidden_conv, 'frame', axis=3, tiled=True)  6.06 us
    dot_general x18, matrix products, conv_tile(): jnp.einsum('nci,coi->no', stacked.reshape(-1, 3, width), kernel[shift_tim...  5.73 us
    all_gather x1, blocking collectives, local(): gathered = lax.all_gather(second, 'frame', axis=0, tiled=True)  5.42 us
  transfers between devices with their start and end apart: 9, of which 5 were waited for; matrix products, arithmetic and copies ran while one was open for 6% of the time, Pallas kernels for 0%

profile of v1, /device:TPU:0, one launch (start us, length us, event | category | flops | bytes accessed | tf_op | source)
XLA Modules:
  0.0 129.8 jit_solution(11087425191196350645)
XLA Ops:
  6.5 2.4 %copy.40 = bf16[512,2,512]{2,0,1:T(8,128)(2,1)} copy(bf16[512,2,512]{2,1,0:T(2,128)(2,1)} %param.14) | data formatting | bytes 2097152 | tf_op args[4]
  9.0 0.0 all-gather.5.cloned.1.call-start
  9.0 0.5 collective-permute-start
  9.6 2.0 %collective-permute-start.1 = (bf16[3,128,512]{2,1,0:T(8,128)(2,1)}, bf16[3,128,512]{2,1,0:T(8,128)(2,1)S(1)}, u32[]{:S(2)}, u32[]{:S(2)}) collective-permute-start(bf16[3,128,512]{2,1,0:T(8,128)(2,1)} %param.11), channel_id=1, source_target_pairs={{1,0},{2,1},{3,2},{0,3},{5,4},{6,5},{7,6},{4,7},{9,8},{10,9},{11,1... | collective-permute-start | bytes 1179656 | tf_op jit(solution)/shard_map/ppermute | solution.py:13
  11.6 0.2 convolution_bitcast_fusion.22
  11.9 16.9 %all_gather.15 = bf16[512,512]{1,0:T(8,128)(2,1)S(1)} all-gather(bf16[128,512]{1,0:T(8,128)(2,1)S(1)} %copy-done.3), channel_id=1, replica_groups=mesh['parts'=2,'row'=4,'frame'=4] {'frame'}, dimensions={0}, use_global_device_ids=true | all-gather | bytes 655360 | tf_op jit(solution)/shard_map/all_gather | solution.py:145
  28.8 0.3 collective-permute-start.2
  29.2 0.2 convolution_bitcast_fusion.21
  29.5 0.2 convolution_bitcast_fusion.20
  29.8 15.5 %collective-permute-done.2 = bf16[3,128,512]{2,1,0:T(8,128)(2,1)S(1)} collective-permute-done((bf16[3,128,512]{2,1,0:T(8,128)(2,1)S(1)}, bf16[3,128,512]{2,1,0:T(8,128)(2,1)S(1)}, u32[]{:S(2)}, u32[]{:S(2)}) %collective-permute-start.2) | collective-permute-done | bytes 393248 | tf_op jit(solution)/shard_map/ppermute | solution.py:26
  45.3 0.2 convolution_bitcast_fusion.19
  45.6 0.2 reshape.302
  45.8 0.2 copy.50
  46.0 0.1 maximum_reduce_fusion
  46.2 0.2 fusion.5
  46.3 22.4 %all-reduce.3 = (bf16[1,16,32,32]{3,2,1,0:T(8,128)(2,1)S(1)}, bf16[1,16,32]{2,1,0:T(8,128)(2,1)S(1)}) all-reduce(bf16[1,16,32,32]{3,2,1,0:T(8,128)(2,1)S(1)} %fusion.5, bf16[1,16,32]{2,1,0:T(8,128)(2,1)S(1)} %bitcast.394), channel_id=1, replica_groups=mesh['parts'=2,'row'=4,'frame'=4] {'row'}, use_global_device_ids=true, to_apply=%region_0.1 | all-reduce | flops 16896 | bytes 67584 | tf_op jit(solution)/shard_map/psum | solution.py:65
  68.7 0.2 copy.52
  68.9 0.2 fusion.173
  69.2 0.4 fusion.23
  69.6 0.2 copy.39
  69.7 0.2 reshape.306
  69.9 0.3 multiply_reduce_fusion.1
  70.2 0.1 fusion.183
  70.3 3.1 %multiply_convert_fusion = bf16[2,16,2,2048]{3,1,2,0:T(8,128)(2,1)S(1)} fusion(bf16[512,2,2048]{2,0,1:T(8,128)(2,1)} %all-gather.3.cloned.1.call-done, bf16[1,2,16,512]{3,2,1,0:T(8,128)(2,1)S(1)} %fusion.183), kind=kOutput, calls=%fused_computation.155 | convolution fusion | flops 134873088 | bytes 4489216 | tf_op jit(solution)/shard_map/frwc,ckj->frwkj/dot_general | solution.py:150
  73.5 1.3 collective-permute-start.3
  74.8 1.3 collective-permute-start.4
  76.1 1.2 collective-permute-done.3
  77.3 4.4 %collective-permute-done.4 = bf16[1,1,16,2,2048]{4,2,3,1,0:T(8,128)(2,1)S(1)} collective-permute-done((bf16[1,1,16,2,2048]{4,2,3,1,0:T(8,128)(2,1)S(1)}, bf16[1,1,16,2,2048]{4,2,3,1,0:T(8,128)(2,1)S(1)}, u32[]{:S(2)}, u32[]{:S(2)}) %collective-permute-start.4) | collective-permute-done | bytes 131104 | tf_op jit(solution)/shard_map/ppermute | solution.py:43
  81.6 0.3 fusion.28
  81.9 0.5 fusion.77
  82.4 2.1 %multiply_reduce_fusion = (f32[2,16]{1,0:T(2,128)S(1)}, f32[2,16,512]{2,1,0:T(8,128)S(1)}) fusion(bf16[2048,512]{1,0:T(8,128)(2,1)} %all-gather.5.cloned.1.call-done, f32[1,2,16,2,2048]{4,2,3,1,0:T(8,128)S(1)} %fusion.77), kind=kOutput, calls=%fused_computation.269 | convolution fusion | flops 67534816 | bytes 2687104 | tf_op jit(solution)/shard_map/frwj,jc->frwc/dot_general | solution.py:159
  84.5 0.1 fusion.182
  84.6 5.4 %all_gather.18 = bf16[4,2,16,512]{3,2,1,0:T(8,128)(2,1)S(1)} all-gather(bf16[1,2,16,512]{3,2,1,0:T(8,128)(2,1)S(1)} %fusion.182), channel_id=1, replica_groups=mesh['parts'=2,'row'=4,'frame'=4] {'frame'}, dimensions={0}, use_global_device_ids=true | all-gather | bytes 163840 | tf_op jit(solution)/shard_map/all_gather | solution.py:166
  90.0 3.8 %collective-permute-start.5 = (bf16[4,2,16,512]{3,2,1,0:T(8,128)(2,1)S(1)}, bf16[4,2,16,512]{3,2,1,0:T(8,128)(2,1)S(1)}, u32[]{:S(2)}, u32[]{:S(2)}) collective-permute-start(bf16[4,2,16,512]{3,2,1,0:T(8,128)(2,1)S(1)} %all_gather.18), channel_id=1, source_target_pairs={{0,4},{4,8},{8,12},{1,5},{5,9},{9,13},{2,6},{6,10},{10,14},{3,7},{... | collective-permute-start | bytes 393224 | tf_op jit(solution)/shard_map/ppermute | solution.py:41
  93.8 1.3 collective-permute-start.6
  95.1 1.9 %collective-permute-done.5 = bf16[4,2,16,512]{3,2,1,0:T(8,128)(2,1)S(1)} collective-permute-done((bf16[4,2,16,512]{3,2,1,0:T(8,128)(2,1)S(1)}, bf16[4,2,16,512]{3,2,1,0:T(8,128)(2,1)S(1)}, u32[]{:S(2)}, u32[]{:S(2)}) %collective-permute-start.5) | collective-permute-done | bytes 131104 | tf_op jit(solution)/shard_map/ppermute | solution.py:41
  97.1 4.1 %collective-permute-done.6 = bf16[4,2,16,512]{3,2,1,0:T(8,128)(2,1)S(1)} collective-permute-done((bf16[4,2,16,512]{3,2,1,0:T(8,128)(2,1)S(1)}, bf16[4,2,16,512]{3,2,1,0:T(8,128)(2,1)S(1)}, u32[]{:S(2)}, u32[]{:S(2)}) %collective-permute-start.6) | collective-permute-done | bytes 131104 | tf_op jit(solution)/shard_map/ppermute | solution.py:43
  101.2 0.8 pad_slice_fusion.23
  102.0 0.2 fusion.215
  102.2 1.0 copy-done.6
  103.2 0.4 convolution_bitcast_fusion.8
  103.6 0.4 convolution_bitcast_fusion.7
  104.0 0.4 convolution_bitcast_fusion.6
  104.4 0.4 convolution_bitcast_fusion.5
  104.8 0.4 convolution_bitcast_fusion.4
  105.1 0.4 convolution_bitcast_fusion.3
  105.5 0.4 convolution_bitcast_fusion.2
  105.9 0.4 convolution_bitcast_fusion.1
  106.3 0.4 fusion.13
  106.7 0.1 multiply_convert_fusion.1
  106.7 6.1 %all_gather.19 = bf16[4,4,16,512]{3,2,1,0:T(8,128)(2,1)S(1)} all-gather(bf16[4,4,16,128]{3,2,1,0:T(8,128)(2,1)S(1)} %multiply_convert_fusion.1), channel_id=1, replica_groups=mesh['parts'=2,'row'=4,'frame'=4] {'frame'}, dimensions={3}, use_global_device_ids=true | all-gather | bytes 327680 | tf_op jit(solution)/shard_map/all_gather | solution.py:173
  112.8 0.3 pad_slice_fusion.47
  113.2 0.1 fusion.217
  113.3 0.3 convolution_bitcast_fusion.17
  113.6 0.3 convolution_bitcast_fusion.16
  113.8 0.3 convolution_bitcast_fusion.15
  114.1 0.3 convolution_bitcast_fusion.14
  114.4 0.3 convolution_bitcast_fusion.13
  114.6 0.3 convolution_bitcast_fusion.12
  114.9 0.3 convolution_bitcast_fusion.11
  115.2 0.3 convolution_bitcast_fusion.10
  115.5 0.3 fusion.21
  115.8 6.5 %all_to_all.18 = bf16[4,2,16,128]{3,1,0,2:T(2,128)(2,1)S(1)} all-to-all(bf16[4,2,16,128]{3,1,0,2:T(2,128)(2,1)S(1)} %copy.42), channel_id=1, replica_groups=mesh['parts'=2,'row'=4,'frame'=4] {'frame'}, dimensions={2} | all-to-all | bytes 65536 | tf_op jit(solution)/shard_map/all_to_all | solution.py:177
  122.4 0.6 all_to_all.16
  (42 shorter events, 0.5 us)
Async XLA Ops:
  6.5 5.1 %copy-start.1 = (bf16[3,128,512]{2,1,0:T(8,128)(2,1)S(1)}, bf16[3,128,512]{2,1,0:T(8,128)(2,1)}, u32[]{:S(2)}) copy-start(bf16[3,128,512]{2,1,0:T(8,128)(2,1)} %param.11) | copy-start | bytes 1179652
  6.5 5.1 %copy-start = (bf16[1,2,16,512]{3,2,1,0:T(8,128)(2,1)S(1)}, bf16[1,2,16,512]{3,2,1,0:T(8,128)(2,1)}, u32[]{:S(2)}) copy-start(bf16[1,2,16,512]{3,2,1,0:T(8,128)(2,1)} %param.10) | copy-start | bytes 98308
  6.5 5.4 %copy-start.3 = (bf16[128,512]{1,0:T(8,128)(2,1)S(1)}, bf16[128,512]{1,0:T(8,128)(2,1)}, u32[]{:S(2)}) copy-start(bf16[128,512]{1,0:T(8,128)(2,1)} %param.12) | copy-start | bytes 393220
  6.5 63.8 %all-gather.3.cloned.1.call-start = ((), (), s32[]{:S(2)}) async-start(), calls=%async_computation.1 | async-start | bytes 5242880 | tf_op jit(solution)/shard_map/all_gather | solution.py:153
  9.0 73.4 %all-gather.5.cloned.1.call-start = ((), (), s32[]{:S(2)}) async-start(), calls=%async_computation.2 | async-start | bytes 2621440 | tf_op jit(solution)/shard_map/all_gather | solution.py:162
  9.0 19.8 %collective-permute-start = (bf16[3,128,512]{2,1,0:T(8,128)(2,1)}, bf16[3,128,512]{2,1,0:T(8,128)(2,1)S(1)}, u32[]{:S(2)}, u32[]{:S(2)}) collective-permute-start(bf16[3,128,512]{2,1,0:T(8,128)(2,1)} %param.11), channel_id=1, source_target_pairs={{0,1},{1,2},{2,3},{3,0},{4,5},{5,6},{6,7},{7,4},{8,9},{9,10},{10,1... | collective-permute-start | bytes 1179656 | tf_op jit(solution)/shard_map/ppermute | solution.py:13
  9.6 19.9 %collective-permute-start.1 = (bf16[3,128,512]{2,1,0:T(8,128)(2,1)}, bf16[3,128,512]{2,1,0:T(8,128)(2,1)S(1)}, u32[]{:S(2)}, u32[]{:S(2)}) collective-permute-start(bf16[3,128,512]{2,1,0:T(8,128)(2,1)} %param.11), channel_id=1, source_target_pairs={{1,0},{2,1},{3,2},{0,3},{5,4},{6,5},{7,6},{4,7},{9,8},{10,9},{11,1... | collective-permute-start | bytes 1179656 | tf_op jit(solution)/shard_map/ppermute | solution.py:13
  11.9 58.3 %copy-start.4 = (f32[512]{0:T(512)S(1)}, f32[512]{0:T(512)}, u32[]{:S(2)}) copy-start(f32[512]{0:T(512)} %param.13) | copy-start | bytes 6148
  28.8 16.5 %collective-permute-start.2 = (bf16[3,128,512]{2,1,0:T(8,128)(2,1)S(1)}, bf16[3,128,512]{2,1,0:T(8,128)(2,1)S(1)}, u32[]{:S(2)}, u32[]{:S(2)}) collective-permute-start(bf16[3,128,512]{2,1,0:T(8,128)(2,1)S(1)} %collective-permute-done), channel_id=1, source_target_pairs={{0,1},{1,2},{2,3},{3,0},{4,5},{5,6},{6,7},{7,4},{8,9},{9,10},{10,1... | collective-permute-start | bytes 1179656 | tf_op jit(solution)/shard_map/ppermute | solution.py:26
  70.3 5.8 %copy-start.2 = (f32[3,3,2,2048]{3,2,1,0:T(2,128)S(1)}, f32[3,3,2,2048]{3,2,1,0:T(2,128)}, u32[]{:S(2)}) copy-start(f32[3,3,2,2048]{3,2,1,0:T(2,128)} %param.15) | copy-start | bytes 442372
  73.5 3.8 %collective-permute-start.3 = (bf16[1,1,16,2,2048]{4,2,3,1,0:T(8,128)(2,1)S(1)}, bf16[1,1,16,2,2048]{4,2,3,1,0:T(8,128)(2,1)S(1)}, u32[]{:S(2)}, u32[]{:S(2)}) collective-permute-start(bf16[1,1,16,2,2048]{4,2,3,1,0:T(8,128)(2,1)S(1)} %get-tuple-element.62), channel_id=1, source_target_pairs={{0,4},{4,8},{8,12},{1,5},{5,9},{9,13},{2,6},{6,10},{10,14},{3,7},{... | collective-permute-start | bytes 393224 | tf_op jit(solution)/shard_map/ppermute | solution.py:41
  74.8 6.9 %collective-permute-start.4 = (bf16[1,1,16,2,2048]{4,2,3,1,0:T(8,128)(2,1)S(1)}, bf16[1,1,16,2,2048]{4,2,3,1,0:T(8,128)(2,1)S(1)}, u32[]{:S(2)}, u32[]{:S(2)}) collective-permute-start(bf16[1,1,16,2,2048]{4,2,3,1,0:T(8,128)(2,1)S(1)} %get-tuple-element.63), channel_id=1, source_target_pairs={{4,0},{8,4},{12,8},{5,1},{9,5},{13,9},{6,2},{10,6},{14,10},{7,3},{... | collective-permute-start | bytes 393224 | tf_op jit(solution)/shard_map/ppermute | solution.py:43
  76.1 8.4 %copy-start.5 = (f32[512]{0:T(512)S(1)}, f32[512]{0:T(512)}, u32[]{:S(2)}) copy-start(f32[512]{0:T(512)} %param.17) | copy-start | bytes 6148
  90.0 7.0 %collective-permute-start.5 = (bf16[4,2,16,512]{3,2,1,0:T(8,128)(2,1)S(1)}, bf16[4,2,16,512]{3,2,1,0:T(8,128)(2,1)S(1)}, u32[]{:S(2)}, u32[]{:S(2)}) collective-permute-start(bf16[4,2,16,512]{3,2,1,0:T(8,128)(2,1)S(1)} %all_gather.18), channel_id=1, source_target_pairs={{0,4},{4,8},{8,12},{1,5},{5,9},{9,13},{2,6},{6,10},{10,14},{3,7},{... | collective-permute-start | bytes 393224 | tf_op jit(solution)/shard_map/ppermute | solution.py:41
  93.8 7.4 %collective-permute-start.6 = (bf16[4,2,16,512]{3,2,1,0:T(8,128)(2,1)S(1)}, bf16[4,2,16,512]{3,2,1,0:T(8,128)(2,1)S(1)}, u32[]{:S(2)}, u32[]{:S(2)}) collective-permute-start(bf16[4,2,16,512]{3,2,1,0:T(8,128)(2,1)S(1)} %all_gather.18), channel_id=1, source_target_pairs={{4,0},{8,4},{12,8},{5,1},{9,5},{13,9},{6,2},{10,6},{14,10},{7,3},{... | collective-permute-start | bytes 393224 | tf_op jit(solution)/shard_map/ppermute | solution.py:43
  101.2 2.0 %copy-start.6 = (bf16[3,3,3,128,512]{4,3,2,1,0:T(8,128)(2,1)S(1)}, bf16[3,3,3,128,512]{4,3,2,1,0:T(8,128)(2,1)}, u32[]{:S(2)}) copy-start(bf16[3,3,3,128,512]{4,3,2,1,0:T(8,128)(2,1)} %param.18) | copy-start | bytes 10616836
  106.3 7.0 %copy-start.7 = (bf16[3,3,3,128,512]{4,3,2,1,0:T(8,128)(2,1)S(1)}, bf16[3,3,3,128,512]{4,3,2,1,0:T(8,128)(2,1)}, u32[]{:S(2)}) copy-start(bf16[3,3,3,128,512]{4,3,2,1,0:T(8,128)(2,1)} %param.19) | copy-start | bytes 10616836
Sparse Core Ops, SparseCore 0:
  9.1 43.3 all-gather.2
  54.0 24.6 all-gather.4
